TPU v7x, 32 devices: a whole 2x2x4 slice. The times are simulated.
32 devices in a mesh: grp: 4 (over y, x), slab: 8 (over z, core).
Axes of the slice: x: 2, y: 2, z: 4, core: 2. Of those that a mesh axis runs over, the one named last changes fastest.
Arguments:
- fields: float32 [64, 64, 8, 128], P('grp', 'slab'), may hold values from -6 to 6
- velocity: int32 [3, 64, 8, 128], P(None, 'slab'), may hold values from -2 to 2
- diffusivity: float32 [64, 8, 128], P('slab'), may hold values from 0.005 to 0.04
- sensor_offsets: int32 [49152], P('slab'), may hold values from 0 to 8191
- sensor_counts: int32 [8], P('slab'), may hold values from 1 to 6144, 16384 in all
- observations: float32 [49152], P('slab'), may hold values from -6 to 6
- noise_scale: float32 [49152], P('slab'), may hold values from 2 to 20
- perturbation: float32 [64, 49152], P('grp', 'slab'), may hold values from -6 to 6
Outputs:
- updated: float32 [64, 64, 8, 128], P('grp', 'slab')
Inputs may be any that keep to these rules, and one draw needn't show every extreme that they name: `sensor_counts`: the counts sum to 16384 and the largest is exactly 6144. `sensor_offsets`: slots at or past their slab's count are unused.
All inputs are finite; a program needn't handle non-finite values. No bound on the sum of `sensor_counts` on one device may be relied on, other than what follows from the above.
Results may differ from a plain program's by a relative error of at most 0.00011.
Values sent between devices are 32-bit elements; how exact they have to be, the bound alone decides.
A program may use at most 64 MiB of HBM per device.

v0:
```python
import math
import jax
import jax.numpy as jnp
from jax import lax
from jax.sharding import PartitionSpec as P

STEPS = 2
COURANT = 0.12


def extended_2(array, sides, width):
    for axis, dim in sides:
        size, length = (lax.axis_size(axis), array.shape[dim])
        up = [(i, (i + 1) % size) for i in range(size - 1)]
        down = [(j, i) for i, j in up]
        last = lax.slice_in_dim(array, length - width, length, axis=dim)
        initial = lax.slice_in_dim(array, 0, width, axis=dim)
        before = lax.ppermute(last, axis, up)
        after = lax.ppermute(initial, axis, down)
        array = jnp.concatenate([before, array, after], axis=dim)
    return array


def upwind(courant, center, lower_side, upper_side):
    return jnp.maximum(courant, 0.0) * (center - lower_side) + jnp.minimum(courant, 0.0) * (
        upper_side - center
    )


def advance(extended, courant, diffusivity):
    center = extended[:, 1:-1]
    below = extended[:, :-2]
    above = extended[:, 2:]
    south = jnp.roll(center, 1, axis=2)
    north = jnp.roll(center, -1, axis=2)
    west = jnp.roll(center, 1, axis=3)
    east = jnp.roll(center, -1, axis=3)
    transport = upwind(courant[0], center, below, above) + upwind(courant[1], center, south, north)
    transport = transport + upwind(courant[2], center, west, east)
    laplace = below + above + south + north + west + east - 6.0 * center
    return center - transport + diffusivity * laplace


def solve_weights(gram_matrix, cross_matrix, spread_root):
    order = gram_matrix.shape[0]
    index_row = jnp.arange(order, dtype=jnp.int32)
    system = jnp.eye(order, dtype=jnp.float32) + gram_matrix

    def factor_column(column, lower_factor):
        row_here = lax.dynamic_slice_in_dim(lower_factor, column, 1, 0)[0]
        needed = lax.dynamic_slice_in_dim(system, column, 1, 1)[:, 0]
        needed = needed - jnp.dot(
            lower_factor,
            row_here,
            precision=lax.Precision.HIGHEST,
            preferred_element_type=jnp.float32,
        )
        pivot = jnp.sqrt(lax.dynamic_slice_in_dim(needed, column, 1, 0)[0])
        values = jnp.where(index_row >= column, needed / pivot, 0.0)
        marker = (index_row == column).astype(jnp.float32)
        return lower_factor + values[:, None] * marker[None, :]

    lower_factor = lax.fori_loop(0, order, factor_column, jnp.zeros((order, order), jnp.float32))

    def forward_row(row, solved):
        factor_row = lax.dynamic_slice_in_dim(lower_factor, row, 1, 0)[0]
        pivot = lax.dynamic_slice_in_dim(factor_row, row, 1, 0)[0]
        given = lax.dynamic_slice_in_dim(cross_matrix, row, 1, 0)[0]
        value = (
            given
            - jnp.dot(
                factor_row,
                solved,
                precision=lax.Precision.HIGHEST,
                preferred_element_type=jnp.float32,
            )
        ) / pivot
        return lax.dynamic_update_slice_in_dim(solved, value[None, :], row, 0)

    middle = lax.fori_loop(0, order, forward_row, jnp.zeros_like(cross_matrix))

    def backward_row(turn, solved):
        row = order - 1 - turn
        factor_col = lax.dynamic_slice_in_dim(lower_factor, row, 1, 1)[:, 0]
        pivot = lax.dynamic_slice_in_dim(factor_col, row, 1, 0)[0]
        given = lax.dynamic_slice_in_dim(middle, row, 1, 0)[0]
        value = (
            given
            - jnp.dot(
                factor_col,
                solved,
                precision=lax.Precision.HIGHEST,
                preferred_element_type=jnp.float32,
            )
        ) / pivot
        return lax.dynamic_update_slice_in_dim(solved, value[None, :], row, 0)

    result = lax.fori_loop(0, order, backward_row, jnp.zeros_like(cross_matrix))
    return result / spread_root


def ensemble_parts(centered, misfit_rows):
    gram_part = jnp.dot(
        centered, centered.T, precision=lax.Precision.HIGHEST, preferred_element_type=jnp.float32
    )
    cross_part = jnp.dot(
        centered, misfit_rows.T, precision=lax.Precision.HIGHEST, preferred_element_type=jnp.float32
    )
    return (gram_part, cross_part)


def sample_cells(current, sensor_offsets):
    members_here = current.shape[0]
    row_count = current.shape[1] * current.shape[2]
    width = current.shape[3]
    planes = current.reshape(members_here, row_count, width)
    slot_total = sensor_offsets.shape[0]
    block_size = math.gcd(slot_total, 512)
    block_count = slot_total // block_size
    row_ids = jnp.arange(row_count, dtype=jnp.int32)
    col_ids = jnp.arange(width, dtype=jnp.int32)

    def pick_block(offsets):
        row_pick = offsets // width
        col_pick = offsets % width
        col_table = (col_ids[:, None] == col_pick[None, :]).astype(jnp.float32)
        chosen = jnp.einsum(
            "qng,gl->qnl",
            planes,
            col_table,
            precision=lax.Precision.HIGHEST,
            preferred_element_type=jnp.float32,
        )
        row_table = (row_ids[:, None] == row_pick[None, :]).astype(jnp.float32)
        return jnp.sum(chosen * row_table[None, :, :], axis=1)

    blocks = lax.map(pick_block, sensor_offsets.reshape(block_count, block_size))
    return jnp.transpose(blocks, (1, 0, 2)).reshape(members_here, slot_total)


def local(
    fields,
    velocity,
    diffusivity,
    sensor_offsets,
    sensor_counts,
    observations,
    noise_scale,
    perturbation,
):
    members_here = fields.shape[0]
    group_count = lax.axis_size("grp")
    members_all = members_here * group_count
    spread_root = math.sqrt(members_all - 1)
    courant = velocity.astype(jnp.float32) * COURANT
    current = fields
    for counter in range(STEPS):
        extended = extended_2(current, (("slab", 1),), 1)
        current = advance(extended, courant, diffusivity)
    cell_total = current.shape[1] * current.shape[2] * current.shape[3]
    flattened = current.reshape(members_here, cell_total)
    slot_total = sensor_offsets.shape[0]
    live_mask = (jnp.arange(slot_total, dtype=jnp.int32) < sensor_counts[0]).astype(jnp.float32)
    predicted = sample_cells(current, sensor_offsets)
    scaled = live_mask * predicted / noise_scale
    misfit = live_mask * ((observations - predicted) / noise_scale + perturbation)
    scaled_sum = lax.psum(jnp.sum(scaled, axis=0), "grp")
    leading = (scaled - scaled_sum / members_all) / spread_root
    gathered_lead, gathered_misfit = (
        lax.all_gather(leading, "grp", axis=0, tiled=True),
        lax.all_gather(misfit, "grp", axis=0, tiled=True),
    )
    gram_part, cross_part = ensemble_parts(gathered_lead, gathered_misfit)
    gram_matrix, cross_matrix = lax.psum((gram_part, cross_part), "slab")
    weights = solve_weights(gram_matrix, cross_matrix, spread_root)
    group_index = lax.axis_index("grp")
    own_weights = lax.dynamic_slice_in_dim(weights, group_index * members_here, members_here, 1)
    increment = jnp.dot(
        own_weights.T,
        lax.all_gather(flattened, "grp", axis=0, tiled=True),
        precision=lax.Precision.HIGHEST,
        preferred_element_type=jnp.float32,
    )
    return (flattened + increment).reshape(current.shape)


def solution(mesh):
    return jax.shard_map(
        local,
        mesh=mesh,
        in_specs=(
            P("grp", "slab", None, None),
            P(None, "slab", None, None),
            P("slab", None, None),
            P("slab"),
            P("slab"),
            P("slab"),
            P("slab"),
            P("grp", "slab"),
        ),
        out_specs=P("grp", "slab", None, None),
        check_vma=False,
    )
```

profile of v0, /device:TPU:0, one launch (start us, length us, event | category | flops | bytes accessed | tf_op | source)
XLA Modules:
  0.0 487.9 jit_solution(3557998516879532501)
XLA Ops:
  6.5 1.6 fusion.75
  8.1 3.0 collective-permute-start
  11.1 1.3 collective-permute-start.1
  12.4 1.3 fusion.72
  17.3 1.3 reshape.81
  19.9 1.4 div.111
  21.9 2.0 fusion.51
  24.5 4.6 collective-permute-start.2
  29.1 1.3 collective-permute-start.3
  30.5 3.0 collective-permute-done.3
  34.4 31.0 %while.62 = (s32[]{:T(128)}, f32[12,16,512]{2,1,0:T(8,128)S(1)}, s32[12,512]{1,0:T(8,128)}, f32[16,64,128]{2,1,0:T(8,128)S(1)}, s32[]{:T(128)}) while((s32[]{:T(128)}, f32[12,16,512]{2,1,0:T(8,128)S(1)}, s32[12,512]{1,0:T(8,128)}, f32[16,64,128]{2,1,0:T(8,128)S(1)}, s32[]{:T(128)}) %tuple.168), condition=%wide.region_2.3_spmd.clone, body=%wide.region_0.2_spmd.clone.sunk | while | flops 806489600 | bytes 901193 | solution.py:137
  35.9 1.0 fusion.109
  38.5 1.0 fusion.109
  41.1 1.0 fusion.109
  43.7 1.0 fusion.109
  46.3 1.0 fusion.109
  48.9 1.1 fusion.109
  51.5 1.0 fusion.109
  56.6 1.0 fusion.109
  59.2 1.1 fusion.109
  64.4 1.0 fusion.109
  65.7 16.3 %psum.21 = f32[6144]{0:T(1024)S(1)} all-reduce(f32[6144]{0:T(1024)S(1)} %reduce_sum.24), channel_id=1, replica_groups=mesh['grp'=4,'slab'=8] {'grp'}, use_global_device_ids=true, to_apply=%region_4.5 | all-reduce | flops 6144 | bytes 49152 | tf_op jit(solution)/shard_map/psum | solution.py:167
  83.8 1.1 copy.20
  85.0 29.7 %all-gather.4.cloned.1.call-done = f32[64,6144]{1,0:T(8,128)} async-done(((f32[16,6144]{1,0:T(8,128)}), f32[64,6144]{1,0:T(8,128)}) %all-gather.4.cloned.1.call-update) | async-done | bytes 1572880 | tf_op jit(solution)/shard_map/all_gather | solution.py:170
  114.6 3.4 fusion.77
  118.0 29.3 %all-gather.6.cloned.1.call-done = f32[64,6144]{1,0:T(8,128)} async-done(((f32[16,6144]{1,0:T(8,128)}), f32[64,6144]{1,0:T(8,128)}) %all-gather.6.cloned.1.call-update) | async-done | bytes 1572880 | tf_op jit(solution)/shard_map/all_gather | solution.py:171
  147.3 2.8 fusion.76
  150.1 28.9 %all-reduce = (f32[64,64]{1,0:T(8,128)S(1)}, f32[64,64]{1,0:T(8,128)S(1)}) all-reduce(f32[64,64]{1,0:T(8,128)S(1)} %fusion.76, f32[64,64]{1,0:T(8,128)S(1)} %fusion.77), channel_id=1, replica_groups=mesh['grp'=4,'slab'=8] {'slab'}, use_global_device_ids=true, to_apply=%region_8.9 | all-reduce | flops 8192 | bytes 65536 | tf_op jit(solution)/shard_map/psum | solution.py:174
  179.1 105.9 %while.63 = (s32[]{:T(128)}, f32[64,64]{1,0:T(8,128)S(1)}, f32[64,64]{0,1:T(8,128)S(1)}, s32[]{:T(128)}, s32[]{:T(128)}) while((s32[]{:T(128)}, f32[64,64]{1,0:T(8,128)S(1)}, f32[64,64]{0,1:T(8,128)S(1)}, s32[]{:T(128)}, s32[]{:T(128)}) %tuple.153), condition=%wide.region_7.8_spmd.clone.clone, body=%wide.region_6.7_spmd.clone.clone.sunk | while | flops 65923 | bytes 101992 | solution.py:63
  285.1 96.0 %while.60 = (s32[]{:T(128)}, f32[64,64]{1,0:T(8,128)S(1)}, f32[64,64]{1,0:T(8,128)S(1)}, f32[64,64]{1,0:T(8,128)S(1)}, s32[]{:T(128)}, /*index=5*/s32[]{:T(128)}, s32[]{:T(128)}) while((s32[]{:T(128)}, f32[64,64]{1,0:T(8,128)S(1)}, f32[64,64]{1,0:T(8,128)S(1)}, f32[64,64]{1,0:T(8,128)S(1)}, s32[]{:T(128)}, /*index=5*/s32[]{:T(128)}, ...), condition=%wide.region_10.11_spmd, body=%wide.region_9.10_spmd.sunk | while | flops 49283 | bytes 36205 | solution.py:80
  381.1 96.4 %while.61 = (s32[]{:T(128)}, f32[64,64]{1,0:T(8,128)S(1)}, f32[64,64]{1,0:T(8,128)S(1)}, f32[64,64]{0,1:T(8,128)S(1)}, s32[]{:T(128)}, /*index=5*/s32[]{:T(128)}, s32[]{:T(128)}, s32[]{:T(128)}) while((s32[]{:T(128)}, f32[64,64]{1,0:T(8,128)S(1)}, f32[64,64]{1,0:T(8,128)S(1)}, f32[64,64]{0,1:T(8,128)S(1)}, s32[]{:T(128)}, ...), condition=%wide.region_12.13_spmd, body=%wide.region_11.12_spmd.sunk | while | flops 49287 | bytes 35751 | solution.py:98
  477.6 2.9 fusion.26
  (884 shorter events, 277.6 us)
Async XLA Ops:
  6.5 7.2 %copy-start = (f32[16,8,8,128]{3,2,1,0:T(8,128)S(1)}, f32[16,8,8,128]{3,2,1,0:T(8,128)}, u32[]{:S(2)}) copy-start(f32[16,8,8,128]{3,2,1,0:T(8,128)} %param.16) | copy-start | bytes 1572868
  6.5 108.1 %all-gather.4.cloned.1.call-start = ((), (), s32[]{:S(2)}) async-start(), calls=%async_computation | async-start | bytes 1966080 | tf_op jit(solution)/shard_map/all_gather | solution.py:170
  8.1 13.8 %collective-permute-start = (f32[16,1,8,128]{3,2,1,0:T(8,128)}, f32[16,1,8,128]{3,2,1,0:T(8,128)}, u32[]{:S(2)}, u32[]{:S(2)}) collective-permute-start(f32[16,1,8,128]{3,2,1,0:T(8,128)} %get-tuple-element.525), channel_id=1, source_target_pairs={{0,1},{1,2},{2,3},{3,4},{4,5},{5,6},{6,7},{8,9},{9,10},{10,11},{11... | collective-permute-start | bytes 196616 | tf_op jit(solution)/shard_map/ppermute | solution.py:18
  11.1 10.7 %collective-permute-start.1 = (f32[16,1,8,128]{3,2,1,0:T(8,128)}, f32[16,1,8,128]{3,2,1,0:T(8,128)}, u32[]{:S(2)}, u32[]{:S(2)}) collective-permute-start(f32[16,1,8,128]{3,2,1,0:T(8,128)} %get-tuple-element.526), channel_id=1, source_target_pairs={{1,0},{2,1},{3,2},{4,3},{5,4},{6,5},{7,6},{9,8},{10,9},{11,10},{12... | collective-permute-start | bytes 196616 | tf_op jit(solution)/shard_map/ppermute | solution.py:19
  24.2 9.3 %copy-start.3 = (f32[8,8,128]{2,1,0:T(8,128)S(1)}, f32[8,8,128]{2,1,0:T(8,128)}, u32[]{:S(2)}) copy-start(f32[8,8,128]{2,1,0:T(8,128)} %get-tuple-element.529) | copy-start | bytes 98308
  24.2 9.3 %copy-start.4 = (f32[8,8,128]{2,1,0:T(8,128)S(1)}, f32[8,8,128]{2,1,0:T(8,128)}, u32[]{:S(2)}) copy-start(f32[8,8,128]{2,1,0:T(8,128)} %get-tuple-element.530) | copy-start | bytes 98308
  24.2 9.3 %copy-start.5 = (f32[8,8,128]{2,1,0:T(8,128)S(1)}, f32[8,8,128]{2,1,0:T(8,128)}, u32[]{:S(2)}) copy-start(f32[8,8,128]{2,1,0:T(8,128)} %get-tuple-element.531) | copy-start | bytes 98308
  24.2 9.3 %copy-start.6 = (f32[8,8,128]{2,1,0:T(8,128)S(1)}, f32[8,8,128]{2,1,0:T(8,128)}, u32[]{:S(2)}) copy-start(f32[8,8,128]{2,1,0:T(8,128)} %get-tuple-element.532) | copy-start | bytes 98308
  24.3 9.3 %copy-start.7 = (f32[8,8,128]{2,1,0:T(8,128)S(1)}, f32[8,8,128]{2,1,0:T(8,128)}, u32[]{:S(2)}) copy-start(f32[8,8,128]{2,1,0:T(8,128)} %get-tuple-element.533) | copy-start | bytes 98308
  24.3 9.3 %copy-start.8 = (f32[8,8,128]{2,1,0:T(8,128)S(1)}, f32[8,8,128]{2,1,0:T(8,128)}, u32[]{:S(2)}) copy-start(f32[8,8,128]{2,1,0:T(8,128)} %get-tuple-element.534) | copy-start | bytes 98308
  24.3 9.3 %copy-start.9 = (f32[8,8,128]{2,1,0:T(8,128)S(1)}, f32[8,8,128]{2,1,0:T(8,128)}, u32[]{:S(2)}) copy-start(f32[8,8,128]{2,1,0:T(8,128)} %param.18) | copy-start | bytes 98308
  24.5 6.0 %collective-permute-start.2 = (f32[16,1,8,128]{3,2,1,0:T(8,128)S(1)}, f32[16,1,8,128]{3,2,1,0:T(8,128)S(1)}, u32[]{:S(2)}, u32[]{:S(2)}) collective-permute-start(f32[16,1,8,128]{3,2,1,0:T(8,128)S(1)} %get-tuple-element.515), channel_id=1, source_target_pairs={{0,1},{1,2},{2,3},{3,4},{4,5},{5,6},{6,7},{8,9},{9,10},{10,11},{11... | collective-permute-start | bytes 196616 | tf_op jit(solution)/shard_map/ppermute | solution.py:18
  29.1 4.4 collective-permute-start.3
  34.4 31.1 %copy-start.10 = (f32[12,512]{1,0:T(8,128)S(1)}, f32[12,512]{1,0:T(8,128)}, u32[]{:S(2)}) copy-start(f32[12,512]{1,0:T(8,128)} %fusion.61) | copy-start | bytes 73732
  34.4 31.1 %copy-start.11 = (f32[12,512]{1,0:T(8,128)S(1)}, f32[12,512]{1,0:T(8,128)}, u32[]{:S(2)}) copy-start(f32[12,512]{1,0:T(8,128)} %div.111) | copy-start | bytes 73732
  34.4 47.5 %copy-start.12 = (f32[6144]{0:T(1024)S(1)}, f32[6144]{0:T(1024)}, u32[]{:S(2)}) copy-start(f32[6144]{0:T(1024)} %param.22) | copy-start | bytes 73732
  34.4 47.5 %copy-start.13 = (f32[6144]{0:T(1024)S(1)}, f32[6144]{0:T(1024)}, u32[]{:S(2)}) copy-start(f32[6144]{0:T(1024)} %fusion.62) | copy-start | bytes 73732
  34.4 47.5 %copy-start.14 = (f32[6144]{0:T(1024)S(1)}, f32[6144]{0:T(1024)}, u32[]{:S(2)}) copy-start(f32[6144]{0:T(1024)} %param.21) | copy-start | bytes 73732
  65.5 16.5 %copy-start.2 = (f32[16,6144]{1,0:T(8,128)S(1)}, f32[16,6144]{1,0:T(8,128)}, u32[]{:S(2)}) copy-start(f32[16,6144]{1,0:T(8,128)} %param.23) | copy-start | bytes 1179652
  83.0 64.3 %all-gather.6.cloned.1.call-start = ((), (), s32[]{:S(2)}) async-start(), calls=%async_computation.1 | async-start | bytes 1966080 | tf_op jit(solution)/shard_map/all_gather | solution.py:171
  83.8 393.8 %all-gather.8.cloned.1.call-start = ((), (), s32[]{:S(2)}) async-start(), calls=%async_computation.2 | async-start | bytes 2621440 | tf_op jit(solution)/shard_map/all_gather | solution.py:180
  114.6 32.7 %copy-start.1 = (f32[64,6144]{1,0:T(8,128)S(1)}, f32[64,6144]{1,0:T(8,128)}, u32[]{:S(2)}) copy-start(f32[64,6144]{1,0:T(8,128)} %all-gather.4.cloned.1.call-done) | copy-start | bytes 4718596
Sparse Core Ops, SparseCore 0:
  83.1 31.4 all-gather.3
  116.5 30.8 all-gather.5
  149.2 35.2 all-gather.7
where the time goes:
time: 492 us; the launch traced here: 488 us
  local copies, waits for them, and re-layouts  140 us (28%)
  matrix products  134 us (27%)
  waiting for transfers between devices  62.7 us (13%)
  loops' own time  50.6 us (10%)
  blocking collectives  45.2 us (9%)
  other arithmetic  30.7 us (6%)
  between operations  14.2 us (3%)
  starting transfers between devices  10.3 us (2%)
    dot_general x64, matrix products, forward_row(): jnp.dot(factor_row, solved, precision=lax.Precision.HIGHEST, preferred_el...  51.5 us
    dot_general x64, matrix products, backward_row(): jnp.dot(factor_col, solved, precision=lax.Precision.HIGHEST, preferred_el...  51.5 us
    another operation x1, loops' own time, solve_weights(): lax.fori_loop(0, order, factor_column, jnp.zeros((order, order), jnp.floa...  47.1 us
    dynamic_slice x64, local copies, waits for them, and re-layouts, factor_column(): pivot = jnp.sqrt(lax.dynamic_slice_in_dim(needed, column, 1, 0)[0])  43.5 us
    dynamic_slice x64, local copies, waits for them, and re-layouts, forward_row(): pivot = lax.dynamic_slice_in_dim(factor_row, row, 1, 0)[0]  41.6 us
    dynamic_slice x64, local copies, waits for them, and re-layouts, backward_row(): pivot = lax.dynamic_slice_in_dim(factor_col, row, 1, 0)[0]  41.6 us
    all_gather x1, waiting for transfers between devices, local(): lax.all_gather(leading, 'grp', axis=0, tiled=True)  29.7 us
    all_gather x1, waiting for transfers between devices, local(): lax.all_gather(misfit, 'grp', axis=0, tiled=True)  29.3 us
  transfers between devices with their start and end apart: 7, of which 3 were waited for; matrix products, arithmetic and copies ran while one was open for 54% of the time, Pallas kernels for 0%

commit v1 on v0

--- a/solution.py
+++ b/solution.py
@@ -148,6 +148,23 @@
     noise_scale,
     perturbation,
 ):
+
+    def _get_surface(vals, at_axis):
+        mesh_dim = "grp"
+        n_peers_all = lax.axis_size(mesh_dim)
+        tray = [(dd, (dd + 1) % n_peers_all) for dd in range(n_peers_all)]
+        pile = [(dd, (dd - 1) % n_peers_all) for dd in range(n_peers_all)]
+        mat_out, heard = ([vals], [vals])
+        for _ in range(n_peers_all // 2):
+            mat_out.append(lax.ppermute(mat_out[-1], mesh_dim, tray))
+        for _ in range((n_peers_all - 1) // 2):
+            heard.append(lax.ppermute(heard[-1], mesh_dim, pile))
+        return jnp.roll(
+            jnp.concatenate([*mat_out[::-1], *heard[1:]], axis=at_axis),
+            (lax.axis_index(mesh_dim) - n_peers_all // 2) * vals.shape[at_axis],
+            axis=at_axis,
+        )
+
     members_here = fields.shape[0]
     group_count = lax.axis_size("grp")
     members_all = members_here * group_count
@@ -167,7 +184,7 @@
     scaled_sum = lax.psum(jnp.sum(scaled, axis=0), "grp")
     leading = (scaled - scaled_sum / members_all) / spread_root
     gathered_lead, gathered_misfit = (
-        lax.all_gather(leading, "grp", axis=0, tiled=True),
+        _get_surface(leading, 0),
         lax.all_gather(misfit, "grp", axis=0, tiled=True),
     )
     gram_part, cross_part = ensemble_parts(gathered_lead, gathered_misfit)

time: 492 us -> 436 us (0.89)
  waiting for transfers between devices: 62.7 us -> 37.9 us
  matrix products: 134 us -> 119 us
  local copies, waits for them, and re-layouts: 140 us -> 130 us
  loops' own time: 50.6 us -> 43.9 us
    ppermute x0 -> x3, waiting for transfers between devices: none -> 34.8 us  [the longest x2 21.2 us: _get_surface(): mat_out.append(lax.ppermute(mat_out[-1], mesh_dim, tray))]
    all_gather x1 -> x0, waiting for transfers between devices: 29.7 us -> none  [local(): lax.all_gather(leading, 'grp', axis=0, tiled=True)]
    all_gather x1, waiting for transfers between devices: 29.3 us -> 0.02 us  [local(): lax.all_gather(misfit, 'grp', axis=0, tiled=True)]
    another operation x1, loops' own time: 47.1 us -> 40.5 us  [solve_weights(): lax.fori_loop(0, order, factor_column, jnp.zeros((order, order), jnp.floa...]
    dot_general x64, matrix products: 51.5 us -> 44.9 us  [forward_row(): jnp.dot(factor_row, solved, precision=lax.Precision.HIGHEST, preferred_el...]
    dot_general x64, matrix products: 51.5 us -> 44.9 us  [backward_row(): jnp.dot(factor_col, solved, precision=lax.Precision.HIGHEST, preferred_el...]
  transfers between devices with their start and end apart: 7 -> 9, of which waited for: 3 -> 4; matrix products, arithmetic and copies ran while one was open for 54% -> 55% of each run, Pallas kernels for 0% -> 0%
where the time goes in v1:
time: 436 us; the launch traced here: 432 us
  local copies, waits for them, and re-layouts  130 us (30%)
  matrix products  119 us (27%)
  loops' own time  43.9 us (10%)
  blocking collectives  42.6 us (10%)
  waiting for transfers between devices  37.9 us (9%)
  other arithmetic  30.6 us (7%)
  between operations  14.5 us (3%)
  starting transfers between devices  13.2 us (3%)
    dot_general x64, matrix products, forward_row(): jnp.dot(factor_row, solved, precision=lax.Precision.HIGHEST, preferred_el...  44.9 us
    dot_general x64, matrix products, backward_row(): jnp.dot(factor_col, solved, precision=lax.Precision.HIGHEST, preferred_el...  44.9 us
    another operation x1, loops' own time, solve_weights(): lax.fori_loop(0, order, factor_column, jnp.zeros((order, order), jnp.floa...  40.5 us
    dynamic_slice x64, local copies, waits for them, and re-layouts, factor_column(): pivot = jnp.sqrt(lax.dynamic_slice_in_dim(needed, column, 1, 0)[0])  39.1 us
    dynamic_slice x64, local copies, waits for them, and re-layouts, forward_row(): pivot = lax.dynamic_slice_in_dim(factor_row, row, 1, 0)[0]  37.1 us
    dynamic_slice x64, local copies, waits for them, and re-layouts, backward_row(): pivot = lax.dynamic_slice_in_dim(factor_col, row, 1, 0)[0]  37.1 us
    psum x1, blocking collectives, local(): gram_matrix, cross_matrix = lax.psum((gram_part, cross_part), 'slab')  26.3 us
    ppermute x2, waiting for transfers between devices, _get_surface(): mat_out.append(lax.ppermute(mat_out[-1], mesh_dim, tray))  21.2 us
  transfers between devices with their start and end apart: 9, of which 4 were waited for; matrix products, arithmetic and copies ran while one was open for 55% of the time, Pallas kernels for 0%

profile of v1, /device:TPU:0, one launch (start us, length us, event | category | flops | bytes accessed | tf_op | source)
XLA Modules:
  0.0 432.1 jit_solution(11044820400536317919)
XLA Ops:
  6.5 1.6 fusion.81
  8.1 3.0 collective-permute-start
  11.1 1.3 collective-permute-start.1
  12.4 1.3 fusion.78
  13.7 1.4 fusion.79
  18.5 1.3 reshape.81
  21.2 1.4 div.111
  23.1 2.0 fusion.55
  25.8 4.6 %collective-permute-start.2 = (f32[16,1,8,128]{3,2,1,0:T(8,128)S(1)}, f32[16,1,8,128]{3,2,1,0:T(8,128)S(1)}, u32[]{:S(2)}, u32[]{:S(2)}) collective-permute-start(f32[16,1,8,128]{3,2,1,0:T(8,128)S(1)} %get-tuple-element.515), channel_id=1, source_target_pairs={{0,1},{1,2},{2,3},{3,4},{4,5},{5,6},{6,7},{8,9},{9,10},{10,11},{11... | collective-permute-start | bytes 196616 | tf_op jit(solution)/shard_map/ppermute | solution.py:18
  30.4 1.3 collective-permute-start.3
  31.8 3.0 collective-permute-done.3
  35.7 31.1 %while.62 = (s32[]{:T(128)}, f32[12,16,512]{2,1,0:T(8,128)S(1)}, s32[12,512]{1,0:T(8,128)}, f32[16,64,128]{2,1,0:T(8,128)S(1)}, s32[]{:T(128)}) while((s32[]{:T(128)}, f32[12,16,512]{2,1,0:T(8,128)S(1)}, s32[12,512]{1,0:T(8,128)}, f32[16,64,128]{2,1,0:T(8,128)S(1)}, s32[]{:T(128)}) %tuple.166), condition=%wide.region_2.3_spmd.clone, body=%wide.region_0.2_spmd.clone.sunk | while | flops 806489600 | bytes 901193 | solution.py:137
  37.2 1.0 fusion.110
  42.4 1.0 fusion.110
  45.0 1.1 fusion.110
  52.8 1.1 fusion.110
  57.9 1.0 fusion.110
  60.5 1.1 fusion.110
  66.9 16.3 %psum.21 = f32[6144]{0:T(1024)S(1)} all-reduce(f32[6144]{0:T(1024)S(1)} %reduce_sum.24), channel_id=1, replica_groups=mesh['grp'=4,'slab'=8] {'grp'}, use_global_device_ids=true, to_apply=%region_4.5 | all-reduce | flops 6144 | bytes 49152 | tf_op jit(solution)/shard_map/psum | solution.py:184
  84.3 11.2 %collective-permute-done.4 = f32[16,6144]{1,0:T(8,128)S(1)} collective-permute-done((f32[16,6144]{1,0:T(8,128)S(1)}, f32[16,6144]{1,0:T(8,128)S(1)}, u32[]{:S(2)}, u32[]{:S(2)}) %collective-permute-start.4) | collective-permute-done | bytes 393248 | tf_op jit(solution)/shard_map/ppermute | solution.py:159
  95.4 2.9 collective-permute-start.6
  98.4 1.1 copy.20
  99.5 10.0 %collective-permute-done.5 = f32[16,6144]{1,0:T(8,128)S(1)} collective-permute-done((f32[16,6144]{1,0:T(8,128)S(1)}, f32[16,6144]{1,0:T(8,128)S(1)}, u32[]{:S(2)}, u32[]{:S(2)}) %collective-permute-start.5) | collective-permute-done | bytes 393248 | tf_op jit(solution)/shard_map/ppermute | solution.py:159
  109.6 13.6 %collective-permute-done.6 = f32[16,6144]{1,0:T(8,128)S(1)} collective-permute-done((f32[16,6144]{1,0:T(8,128)S(1)}, f32[16,6144]{1,0:T(8,128)S(1)}, u32[]{:S(2)}, u32[]{:S(2)}) %collective-permute-start.6) | collective-permute-done | bytes 393248 | tf_op jit(solution)/shard_map/ppermute | solution.py:161
  123.4 1.6 copy-done.1
  125.1 1.4 fusion.26
  126.5 3.3 fusion.28
  129.8 26.3 %all-reduce = (f32[64,64]{1,0:T(8,128)S(1)}, f32[64,64]{1,0:T(8,128)S(1)}) all-reduce(f32[64,64]{1,0:T(8,128)S(1)} %fusion.28, f32[64,64]{1,0:T(8,128)S(1)} %fusion.26), channel_id=1, replica_groups=mesh['grp'=4,'slab'=8] {'slab'}, use_global_device_ids=true, to_apply=%region_8.9 | all-reduce | flops 8192 | bytes 65536 | tf_op jit(solution)/shard_map/psum | solution.py:191
  156.2 94.8 %while.63 = (s32[]{:T(128)}, f32[64,64]{1,0:T(8,128)S(1)}, f32[64,64]{0,1:T(8,128)S(1)}, s32[]{:T(128)}, s32[]{:T(128)}) while((s32[]{:T(128)}, f32[64,64]{1,0:T(8,128)S(1)}, f32[64,64]{0,1:T(8,128)S(1)}, s32[]{:T(128)}, s32[]{:T(128)}) %tuple.153), condition=%wide.region_7.8_spmd.clone.clone, body=%wide.region_6.7_spmd.clone.clone.sunk | while | flops 65923 | bytes 101992 | solution.py:63
  251.1 84.9 %while.60 = (s32[]{:T(128)}, f32[64,64]{1,0:T(8,128)S(1)}, f32[64,64]{1,0:T(8,128)S(1)}, f32[64,64]{1,0:T(8,128)S(1)}, s32[]{:T(128)}, /*index=5*/s32[]{:T(128)}, s32[]{:T(128)}) while((s32[]{:T(128)}, f32[64,64]{1,0:T(8,128)S(1)}, f32[64,64]{1,0:T(8,128)S(1)}, f32[64,64]{1,0:T(8,128)S(1)}, s32[]{:T(128)}, /*index=5*/s32[]{:T(128)}, ...), condition=%wide.region_10.11_spmd, body=%wide.region_9.10_spmd.sunk | while | flops 49283 | bytes 36205 | solution.py:80
  336.0 85.4 %while.61 = (s32[]{:T(128)}, f32[64,64]{1,0:T(8,128)S(1)}, f32[64,64]{1,0:T(8,128)S(1)}, f32[64,64]{0,1:T(8,128)S(1)}, s32[]{:T(128)}, /*index=5*/s32[]{:T(128)}, s32[]{:T(128)}, s32[]{:T(128)}) while((s32[]{:T(128)}, f32[64,64]{1,0:T(8,128)S(1)}, f32[64,64]{1,0:T(8,128)S(1)}, f32[64,64]{0,1:T(8,128)S(1)}, s32[]{:T(128)}, ...), condition=%wide.region_12.13_spmd, body=%wide.region_11.12_spmd.sunk | while | flops 49287 | bytes 35751 | solution.py:98
  421.5 2.9 fusion.30
  (895 shorter events, 254.5 us)
Async XLA Ops:
  6.5 8.6 %copy-start = (f32[16,8,8,128]{3,2,1,0:T(8,128)S(1)}, f32[16,8,8,128]{3,2,1,0:T(8,128)}, u32[]{:S(2)}) copy-start(f32[16,8,8,128]{3,2,1,0:T(8,128)} %param.16) | copy-start | bytes 1572868
  6.5 119.9 %all-gather.3.cloned.1.call-start = ((), (), s32[]{:S(2)}) async-start(), calls=%async_computation | async-start | bytes 1966080 | tf_op jit(solution)/shard_map/all_gather | solution.py:188
  8.1 15.0 %collective-permute-start = (f32[16,1,8,128]{3,2,1,0:T(8,128)}, f32[16,1,8,128]{3,2,1,0:T(8,128)}, u32[]{:S(2)}, u32[]{:S(2)}) collective-permute-start(f32[16,1,8,128]{3,2,1,0:T(8,128)} %get-tuple-element.525), channel_id=1, source_target_pairs={{0,1},{1,2},{2,3},{3,4},{4,5},{5,6},{6,7},{8,9},{9,10},{10,11},{11... | collective-permute-start | bytes 196616 | tf_op jit(solution)/shard_map/ppermute | solution.py:18
  11.1 12.0 %collective-permute-start.1 = (f32[16,1,8,128]{3,2,1,0:T(8,128)}, f32[16,1,8,128]{3,2,1,0:T(8,128)}, u32[]{:S(2)}, u32[]{:S(2)}) collective-permute-start(f32[16,1,8,128]{3,2,1,0:T(8,128)} %get-tuple-element.526), channel_id=1, source_target_pairs={{1,0},{2,1},{3,2},{4,3},{5,4},{6,5},{7,6},{9,8},{10,9},{11,10},{12... | collective-permute-start | bytes 196616 | tf_op jit(solution)/shard_map/ppermute | solution.py:19
  25.1 9.6 %copy-start.3 = (f32[8,8,128]{2,1,0:T(8,128)S(1)}, f32[8,8,128]{2,1,0:T(8,128)}, u32[]{:S(2)}) copy-start(f32[8,8,128]{2,1,0:T(8,128)} %get-tuple-element.529) | copy-start | bytes 98308
  25.1 9.6 %copy-start.4 = (f32[8,8,128]{2,1,0:T(8,128)S(1)}, f32[8,8,128]{2,1,0:T(8,128)}, u32[]{:S(2)}) copy-start(f32[8,8,128]{2,1,0:T(8,128)} %get-tuple-element.530) | copy-start | bytes 98308
  25.2 9.6 %copy-start.5 = (f32[8,8,128]{2,1,0:T(8,128)S(1)}, f32[8,8,128]{2,1,0:T(8,128)}, u32[]{:S(2)}) copy-start(f32[8,8,128]{2,1,0:T(8,128)} %get-tuple-element.531) | copy-start | bytes 98308
  25.2 9.6 %copy-start.6 = (f32[8,8,128]{2,1,0:T(8,128)S(1)}, f32[8,8,128]{2,1,0:T(8,128)}, u32[]{:S(2)}) copy-start(f32[8,8,128]{2,1,0:T(8,128)} %get-tuple-element.532) | copy-start | bytes 98308
  25.2 9.6 %copy-start.7 = (f32[8,8,128]{2,1,0:T(8,128)S(1)}, f32[8,8,128]{2,1,0:T(8,128)}, u32[]{:S(2)}) copy-start(f32[8,8,128]{2,1,0:T(8,128)} %get-tuple-element.533) | copy-start | bytes 98308
  25.2 9.6 %copy-start.8 = (f32[8,8,128]{2,1,0:T(8,128)S(1)}, f32[8,8,128]{2,1,0:T(8,128)}, u32[]{:S(2)}) copy-start(f32[8,8,128]{2,1,0:T(8,128)} %get-tuple-element.534) | copy-start | bytes 98308
  25.2 9.6 %copy-start.9 = (f32[8,8,128]{2,1,0:T(8,128)S(1)}, f32[8,8,128]{2,1,0:T(8,128)}, u32[]{:S(2)}) copy-start(f32[8,8,128]{2,1,0:T(8,128)} %param.18) | copy-start | bytes 98308
  25.8 6.0 %collective-permute-start.2 = (f32[16,1,8,128]{3,2,1,0:T(8,128)S(1)}, f32[16,1,8,128]{3,2,1,0:T(8,128)S(1)}, u32[]{:S(2)}, u32[]{:S(2)}) collective-permute-start(f32[16,1,8,128]{3,2,1,0:T(8,128)S(1)} %get-tuple-element.515), channel_id=1, source_target_pairs={{0,1},{1,2},{2,3},{3,4},{4,5},{5,6},{6,7},{8,9},{9,10},{10,11},{11... | collective-permute-start | bytes 196616 | tf_op jit(solution)/shard_map/ppermute | solution.py:18
  30.4 4.4 %collective-permute-start.3 = (f32[16,1,8,128]{3,2,1,0:T(8,128)S(1)}, f32[16,1,8,128]{3,2,1,0:T(8,128)S(1)}, u32[]{:S(2)}, u32[]{:S(2)}) collective-permute-start(f32[16,1,8,128]{3,2,1,0:T(8,128)S(1)} %get-tuple-element.516), channel_id=1, source_target_pairs={{1,0},{2,1},{3,2},{4,3},{5,4},{6,5},{7,6},{9,8},{10,9},{11,10},{12... | collective-permute-start | bytes 196616 | tf_op jit(solution)/shard_map/ppermute | solution.py:19
  35.6 31.2 %copy-start.10 = (f32[12,512]{1,0:T(8,128)S(1)}, f32[12,512]{1,0:T(8,128)}, u32[]{:S(2)}) copy-start(f32[12,512]{1,0:T(8,128)} %fusion.65) | copy-start | bytes 73732
  35.6 31.2 %copy-start.11 = (f32[12,512]{1,0:T(8,128)S(1)}, f32[12,512]{1,0:T(8,128)}, u32[]{:S(2)}) copy-start(f32[12,512]{1,0:T(8,128)} %div.111) | copy-start | bytes 73732
  35.7 47.6 %copy-start.2 = (f32[16,6144]{1,0:T(8,128)S(1)}, f32[16,6144]{1,0:T(8,128)}, u32[]{:S(2)}) copy-start(f32[16,6144]{1,0:T(8,128)} %param.23) | copy-start | bytes 1179652
  35.7 47.6 %copy-start.12 = (f32[6144]{0:T(1024)S(1)}, f32[6144]{0:T(1024)}, u32[]{:S(2)}) copy-start(f32[6144]{0:T(1024)} %param.22) | copy-start | bytes 73732
  35.7 47.6 %copy-start.13 = (f32[6144]{0:T(1024)S(1)}, f32[6144]{0:T(1024)}, u32[]{:S(2)}) copy-start(f32[6144]{0:T(1024)} %fusion.66) | copy-start | bytes 73732
  35.7 47.6 %copy-start.14 = (f32[6144]{0:T(1024)S(1)}, f32[6144]{0:T(1024)}, u32[]{:S(2)}) copy-start(f32[6144]{0:T(1024)} %param.21) | copy-start | bytes 73732
  84.2 337.3 %all-gather.5.cloned.1.call-start = ((), (), s32[]{:S(2)}) async-start(), calls=%async_computation.1 | async-start | bytes 2621440 | tf_op jit(solution)/shard_map/all_gather | solution.py:197
  84.2 11.2 %collective-permute-start.4 = (f32[16,6144]{1,0:T(8,128)S(1)}, f32[16,6144]{1,0:T(8,128)S(1)}, u32[]{:S(2)}, u32[]{:S(2)}) collective-permute-start(f32[16,6144]{1,0:T(8,128)S(1)} %get-tuple-element.527), channel_id=1, source_target_pairs={{0,8},{8,16},{16,24},{24,0},{1,9},{9,17},{17,25},{25,1},{2,10},{10... | collective-permute-start | bytes 1179656 | tf_op jit(solution)/shard_map/ppermute | solution.py:159
  95.4 14.1 %collective-permute-start.5 = (f32[16,6144]{1,0:T(8,128)S(1)}, f32[16,6144]{1,0:T(8,128)S(1)}, u32[]{:S(2)}, u32[]{:S(2)}) collective-permute-start(f32[16,6144]{1,0:T(8,128)S(1)} %collective-permute-done.4), channel_id=1, source_target_pairs={{0,8},{8,16},{16,24},{24,0},{1,9},{9,17},{17,25},{25,1},{2,10},{10... | collective-permute-start | bytes 1179656 | tf_op jit(solution)/shard_map/ppermute | solution.py:159
  95.4 27.8 %collective-permute-start.6 = (f32[16,6144]{1,0:T(8,128)S(1)}, f32[16,6144]{1,0:T(8,128)S(1)}, u32[]{:S(2)}, u32[]{:S(2)}) collective-permute-start(f32[16,6144]{1,0:T(8,128)S(1)} %get-tuple-element.527), channel_id=1, source_target_pairs={{0,24},{8,0},{16,8},{24,16},{1,25},{9,1},{17,9},{25,17},{2,26},{10... | collective-permute-start | bytes 1179656 | tf_op jit(solution)/shard_map/ppermute | solution.py:161
  123.4 1.6 copy-start.1
Sparse Core Ops, SparseCore 0:
  84.3 40.5 all-gather.2
  126.7 34.2 all-gather.4
